TPU v7x, 256 devices: a whole 4x4x8 slice. The times are simulated.
256 devices in a mesh: dp: 32 (over y, x, core), mp: 8 (over z).
Axes of the slice: x: 4, y: 4, z: 8, core: 2. Of those that a mesh axis runs over, the one named last changes fastest.
Arguments:
- activations: bfloat16 [4096, 2560], P('dp'), may hold values from -6 to 6
- grad_hidden: bfloat16 [4096, 8192], P('dp', 'mp'), may hold values from -0.059814453 to 0.059814453
- up_weight: bfloat16 [2560, 8192], P('dp', 'mp'), may hold values from -6 to 6
- error_feedback: bfloat16 [32, 2560, 8192], P('dp', None, 'mp'), may hold values from -0.75 to 0.75
- query_previous: float32 [8192, 128], P('mp'), may hold values from -6 to 6
Outputs:
- grad_input: bfloat16 [4096, 2560], P('dp', 'mp')
- error_next: bfloat16 [32, 2560, 8192], P('dp', None, 'mp')
- update: float32 [2560, 8192], P('dp', 'mp')
- query_next: float32 [8192, 128], P('mp')
All inputs are finite; a program needn't handle non-finite values.
Results may differ from a plain program's by a relative error of at most 0.0005.
Values may be sent and summed in bfloat16 or wider, within the bound.
No kernel may reach another device: no remote copies, remote signals or barrier semaphores. Data moves between devices by JAX's collectives and lax.ppermute only.
A program may use at most 128 MiB of HBM per device.

v0:
```python
import jax
import jax.numpy as jnp
from jax import lax
from jax.sharding import PartitionSpec as P

HIGHEST = lax.Precision.HIGHEST


def orthonormal(project, gram_matrix):
    factor = jnp.linalg.cholesky(gram_matrix)
    return lax.linalg.triangular_solve(
        factor, project, left_side=False, lower=True, transpose_a=True
    )


def local(activations, grad_hidden, up_weight, error_feedback, query_previous):
    replicas = lax.axis_size("dp")
    partial_input = lax.dot_general(
        grad_hidden,
        lax.all_gather(up_weight, "dp", axis=0, tiled=True),
        (((1,), (1,)), ((), ())),
        preferred_element_type=jnp.float32,
    )
    grad_input = lax.psum_scatter(partial_input, "mp", scatter_dimension=1, tiled=True).astype(
        jnp.bfloat16
    )
    local_grad = lax.dot_general(
        activations, grad_hidden, (((0,), (0,)), ((), ())), preferred_element_type=jnp.float32
    )
    merged = error_feedback[0].astype(jnp.float32) + local_grad
    project = jnp.dot(merged, query_previous, precision=HIGHEST, preferred_element_type=jnp.float32)
    project = lax.psum(project, ("dp", "mp"))
    gram_matrix = jnp.dot(project.T, project, precision=HIGHEST, preferred_element_type=jnp.float32)
    basis_full = orthonormal(project, gram_matrix)
    query_term = lax.dot_general(
        merged,
        basis_full,
        (((0,), (0,)), ((), ())),
        precision=HIGHEST,
        preferred_element_type=jnp.float32,
    )
    query_next = lax.psum(query_term, "dp") / replicas
    low_rank = lax.dot_general(
        basis_full,
        query_next,
        (((1,), (1,)), ((), ())),
        precision=HIGHEST,
        preferred_element_type=jnp.float32,
    )
    error_next = (merged - low_rank).astype(jnp.bfloat16)[None]
    row_share = merged.shape[0] // replicas
    update = lax.dynamic_slice_in_dim(low_rank, lax.axis_index("dp") * row_share, row_share, 0)
    return (grad_input, error_next, update, query_next)


def solution(mesh):
    in_specs = (P("dp", None), P("dp", "mp"), P("dp", "mp"), P("dp", None, "mp"), P("mp", None))
    out_specs = (P("dp", "mp"), P("dp", None, "mp"), P("dp", "mp"), P("mp", None))
    return jax.shard_map(local, mesh=mesh, in_specs=in_specs, out_specs=out_specs, check_vma=False)
```

profile of v0, /device:TPU:4, one launch (start us, length us, event | category | flops | bytes accessed | tf_op | source)
XLA Modules:
  0.0 501.2 jit_solution(10728935111397148013)
XLA Ops:
  8.0 0.0 copy-start
  8.0 0.0 all-reduce.3.cloned.1.call-start
  8.1 1.0 copy-done
  9.1 0.0 copy-start.5
  9.1 4.2 convert_add_fusion
  13.3 0.0 copy-start.1
  13.3 4.0 copy-done.1
  17.2 0.0 copy-done.5
  17.2 9.4 %fusion.6 = f32[2560,128]{1,0:T(8,128)} fusion(f32[2560,1024]{1,0:T(8,128)S(1)} %convert_add_fusion, f32[1024,128]{1,0:T(8,128)S(1)} %copy-done.5), kind=kOutput, calls=%fused_computation.16 | convolution fusion | flops 4026531840 | bytes 12320768 | tf_op jit(solution)/shard_map/dot_general | solution.py:31
  26.7 0.0 all-reduce.3.cloned.1.call-update
  26.7 0.0 all-gather.2.cloned.1.call-start
  26.7 0.5 all-gather.2.cloned.1.call-update
  27.3 0.5 all-reduce.5.cloned.1.call-start
  27.8 261.2 %all-reduce.3.cloned.1.call-done = f32[2560,128]{1,0:T(8,128)} async-done(((f32[2560,128]{1,0:T(8,128)}), f32[2560,128]{1,0:T(8,128)}) %all-reduce.3.cloned.1.call-update) | async-done | bytes 1310736 | tf_op jit(solution)/shard_map/psum | solution.py:32
  288.9 3.9 fusion.7
  292.9 0.1 copy.9
  293.0 11.7 %cholesky.16 = f32[128,128]{1,0:T(8,128)S(1)} custom-call(f32[128,128]{1,0:T(8,128)S(1)} %fusion.4), custom_call_target="Cholesky" | custom-call | tf_op jit(solution)/shard_map/jit(cholesky)/cholesky | solution.py:10
  304.7 0.6 compare_reduce_fusion
  305.4 0.7 fusion.1
  306.0 9.8 %custom-call.6 = f32[1,128,128]{1,2,0:T(8,128)S(1)} custom-call(f32[1,128,128]{2,1,0:T(8,128)S(1)} %fusion.1), custom_call_target="InvertDiagBlocksLowerTriangular" | custom-call | tf_op jit(solution)/shard_map/triangular_solve | solution.py:11
  315.9 2.5 fusion.2
  318.4 0.0 copy-start.4
  318.4 19.9 %fusion.8 = f32[1024,128]{1,0:T(8,128)} fusion(f32[2560,1024]{1,0:T(8,128)} %copy-done.1, f32[2560,128]{1,0:T(8,128)S(1)} %fusion.2), kind=kOutput, calls=%fused_computation.18 | convolution fusion | flops 4026531840 | bytes 12320768 | tf_op jit(solution)/shard_map/dot_general | solution.py:35
  338.3 0.0 all-reduce.5.cloned.1.call-update
  338.3 0.3 reduce-scatter.2.cloned.1.call-start
  338.6 0.0 all-gather.2.cloned.1.call-done
  338.6 0.0 copy-done.4
  338.6 5.1 %fusion.5 = f32[128,2560]{0,1:T(8,128)} fusion(bf16[128,1024]{1,0:T(8,128)(2,1)S(1)} %copy-done.4, bf16[2560,1024]{1,0:T(8,128)(2,1)} %all-gather.2.cloned.1.call-done), kind=kOutput, calls=%fused_computation.15 | convolution fusion | flops 671088640 | bytes 6815744 | tf_op jit(solution)/shard_map/dot_general | solution.py:18
  343.7 0.0 reduce-scatter.2.cloned.1.call-update
  343.7 106.1 %all-reduce.5.cloned.1.call-done = f32[1024,128]{1,0:T(8,128)} async-done(((f32[1024,128]{1,0:T(8,128)}), f32[1024,128]{1,0:T(8,128)}) %all-reduce.5.cloned.1.call-update) | async-done | bytes 524304 | tf_op jit(solution)/shard_map/psum | solution.py:42
  449.8 1.1 broadcast_multiply_fusion
  450.9 0.0 copy-start.3
  450.9 8.4 %fusion.9 = f32[2560,1024]{1,0:T(8,128)S(1)} fusion(f32[2560,128]{1,0:T(8,128)S(1)} %fusion.2, f32[1024,128]{1,0:T(8,128)S(1)} %broadcast_multiply_fusion), kind=kOutput, calls=%fused_computation.19 | convolution fusion | flops 4026531840 | bytes 12320768 | tf_op jit(solution)/shard_map/dot_general | solution.py:43
  459.4 0.0 copy-done.3
  459.4 0.0 copy-start.2
  459.4 3.8 copy-done.2
  463.2 0.7 constant_dynamic-slice_fusion
  464.0 11.5 %fusion = bf16[1,2560,1024]{2,1,0:T(8,128)(2,1)} fusion(f32[2560,1024]{1,0:T(8,128)} %copy-done.1, f32[2560,1024]{1,0:T(8,128)} %copy-done.2), kind=kLoop, calls=%fused_computation.2 | loop fusion | flops 5242880 | bytes 26214400 | tf_op jit(solution)/shard_map/broadcast_in_dim | solution.py:50
  475.5 16.3 %reduce-scatter.2.cloned.1.call-done = f32[128,320]{0,1:T(8,128)} async-done(((f32[128,2560]{0,1:T(8,128)}), f32[128,320]{0,1:T(8,128)}) %reduce-scatter.2.cloned.1.call-update) | async-done | bytes 163856 | tf_op jit(solution)/shard_map/reduce_scatter | solution.py:24
  491.8 1.6 convert_element_type.12
  (2 shorter events, 0.0 us)
Async XLA Ops:
  8.0 1.1 copy-start
  8.0 280.9 %all-reduce.3.cloned.1.call-start = ((), (), s32[]{:S(2)}) async-start(), calls=%async_computation.3 | async-start | bytes 2621440 | tf_op jit(solution)/shard_map/psum | solution.py:32
  9.1 8.2 %copy-start.5 = (f32[1024,128]{1,0:T(8,128)S(1)}, f32[1024,128]{1,0:T(8,128)}, u32[]{:S(2)}) copy-start(f32[1024,128]{1,0:T(8,128)} %param.9) | copy-start | bytes 1572868
  13.3 4.0 copy-start.1
  26.7 311.9 %all-gather.2.cloned.1.call-start = ((), (), s32[]{:S(2)}) async-start(), calls=%async_computation.1 | async-start | bytes 5406720 | tf_op jit(solution)/shard_map/all_gather | solution.py:20
  27.3 422.5 %all-reduce.5.cloned.1.call-start = ((), (), s32[]{:S(2)}) async-start(), calls=%async_computation.4 | async-start | bytes 1048576 | tf_op jit(solution)/shard_map/psum | solution.py:42
  318.4 20.3 %copy-start.4 = (bf16[128,1024]{1,0:T(8,128)(2,1)S(1)}, bf16[128,1024]{1,0:T(8,128)(2,1)}, u32[]{:S(2)}) copy-start(bf16[128,1024]{1,0:T(8,128)(2,1)} %param.6) | copy-start | bytes 786436
  338.3 153.5 %reduce-scatter.2.cloned.1.call-start = ((), (), s32[]{:S(2)}) async-start(), calls=%async_computation.2 | async-start | bytes 1474560 | tf_op jit(solution)/shard_map/reduce_scatter | solution.py:24
  450.9 8.5 %copy-start.3 = (f32[1024,128]{1,0:T(8,128)}, f32[1024,128]{1,0:T(8,128)S(1)}, u32[]{:S(2)}) copy-start(f32[1024,128]{1,0:T(8,128)S(1)} %broadcast_multiply_fusion) | copy-start | bytes 1572868
  459.4 3.8 copy-start.2
Sparse Core Ops, SparseCore 0:
  26.8 262.0 all-reduce.2
Sparse Core Ops, SparseCore 1:
  29.7 54.2 all-gather.1
  338.4 111.3 all-reduce.4
  452.2 39.5 reduce-scatter.1
where the time goes:
time: 509 us; the launch traced here: 501 us
  waiting for transfers between devices  384 us (75%)
  matrix products  53.5 us (11%)
  other arithmetic  37 us (7%)
  between operations  16 us (3%)
  local copies, waits for them, and re-layouts  9.68 us (2%)
    psum x1, waiting for transfers between devices, local(): project = lax.psum(project, ('dp', 'mp'))  261 us
    psum x1, waiting for transfers between devices, local(): query_next = lax.psum(query_term, 'dp') / replicas  106 us
    dot_general x1, matrix products, local(): lax.dot_general(merged, basis_full, (((0,), (0,)), ((), ())), precision=H...  19.9 us
    reduce_scatter x1, waiting for transfers between devices, local(): lax.psum_scatter(partial_input, 'mp', scatter_dimension=1, tiled=True)  16.3 us
    another operation x3, other arithmetic, orthonormal(): factor = jnp.linalg.cholesky(gram_matrix)  12.4 us
    broadcast_in_dim x1, other arithmetic, local(): error_next = (merged - low_rank).astype(jnp.bfloat16)[None]  11.5 us
    another operation x2, other arithmetic, orthonormal(): lax.linalg.triangular_solve(factor, project, left_side=False, lower=True,...  10.5 us
  transfers between devices with their start and end apart: 4, of which 3 were waited for; matrix products, arithmetic and copies ran while one was open for 15% of the time, Pallas kernels for 0%

commit v1 on v0

--- a/solution.py
+++ b/solution.py
@@ -4,6 +4,7 @@
 from jax.sharding import PartitionSpec as P
 
 HIGHEST = lax.Precision.HIGHEST
+wait_shapes_on = lambda here_x, ax_name: lax.all_gather(here_x, ax_name).sum(axis=0)
 
 
 def orthonormal(project, gram_matrix):
@@ -39,7 +40,7 @@
         precision=HIGHEST,
         preferred_element_type=jnp.float32,
     )
-    query_next = lax.psum(query_term, "dp") / replicas
+    query_next = wait_shapes_on(query_term, "dp") / replicas
     low_rank = lax.dot_general(
         basis_full,
         query_next,

time: 509 us -> 463 us (0.910)
  waiting for transfers between devices: 384 us -> 333 us
  other arithmetic: 37 us -> 42.6 us
    psum x1 -> x0, waiting for transfers between devices: 106 us -> none  [local(): query_next = lax.psum(query_term, 'dp') / replicas]
    all_gather x0 -> x1, waiting for transfers between devices: none -> 74.8 us  [lax.all_gather(here_x, ax_name).sum(axis=0)]
    psum x1, waiting for transfers between devices: 261 us -> 219 us  [local(): project = lax.psum(project, ('dp', 'mp'))]
    all_gather x1, waiting for transfers between devices: 0.02 us -> 38.6 us  [local(): lax.all_gather(up_weight, 'dp', axis=0, tiled=True)]
    reduce_scatter x1, waiting for transfers between devices: 16.3 us -> 0.02 us  [local(): lax.psum_scatter(partial_input, 'mp', scatter_dimension=1, tiled=True)]
    reduce_sum x0 -> x1, other arithmetic: none -> 6.57 us  [lax.all_gather(here_x, ax_name).sum(axis=0)]
where the time goes in v1:
time: 463 us; the launch traced here: 454 us
  waiting for transfers between devices  333 us (72%)
  matrix products  56.1 us (12%)
  other arithmetic  42.6 us (9%)
  between operations  15.5 us (3%)
  local copies, waits for them, and re-layouts  6.08 us (1%)
    psum x1, waiting for transfers between devices, local(): project = lax.psum(project, ('dp', 'mp'))  219 us
    all_gather x1, waiting for transfers between devices, lax.all_gather(here_x, ax_name).sum(axis=0)  74.8 us
    all_gather x1, waiting for transfers between devices, local(): lax.all_gather(up_weight, 'dp', axis=0, tiled=True)  38.6 us
    dot_general x1, matrix products, local(): lax.dot_general(merged, basis_full, (((0,), (0,)), ((), ())), precision=H...  19.9 us
    another operation x3, other arithmetic, orthonormal(): factor = jnp.linalg.cholesky(gram_matrix)  12.4 us
    broadcast_in_dim x1, other arithmetic, local(): error_next = (merged - low_rank).astype(jnp.bfloat16)[None]  11.6 us
    dot_general x1, matrix products, local(): lax.dot_general(basis_full, query_next, (((1,), (1,)), ((), ())), precisi...  11 us
    another operation x2, other arithmetic, orthonormal(): lax.linalg.triangular_solve(factor, project, left_side=False, lower=True,...  10.5 us
  transfers between devices with their start and end apart: 4, of which 3 were waited for; matrix products, arithmetic and copies ran while one was open for 15% of the time, Pallas kernels for 0%

profile of v1, /device:TPU:4, one launch (start us, length us, event | category | flops | bytes accessed | tf_op | source)
XLA Modules:
  0.0 453.8 jit_solution(15477925856506508915)
XLA Ops:
  8.0 0.0 copy-start
  8.0 0.0 all-gather.4.cloned.1.call-start
  8.1 0.7 all-gather.4.cloned.1.call-update
  8.7 0.0 copy-start.4
  8.8 0.0 all-reduce.2.cloned.1.call-start
  8.8 0.3 copy-done
  9.1 4.1 convert_add_fusion
  13.2 0.0 copy-start.1
  13.2 4.0 copy-done.1
  17.2 0.0 copy-done.4
  17.2 0.0 copy-start.3
  17.2 9.4 %fusion.6 = f32[2560,128]{1,0:T(8,128)} fusion(f32[2560,1024]{1,0:T(8,128)S(1)} %convert_add_fusion, f32[1024,128]{1,0:T(8,128)S(1)} %copy-done.4), kind=kOutput, calls=%fused_computation.16 | convolution fusion | flops 4026531840 | bytes 12320768 | tf_op jit(solution)/shard_map/dot_general | solution.py:32
  26.6 0.0 all-reduce.2.cloned.1.call-update
  26.7 0.5 reduce-scatter.2.cloned.1.call-start
  27.2 38.6 %all-gather.4.cloned.1.call-done = bf16[2560,1024]{1,0:T(8,128)(2,1)} async-done(((bf16[80,1024]{1,0:T(8,128)(2,1)}), bf16[2560,1024]{1,0:T(8,128)(2,1)}) %all-gather.4.cloned.1.call-update) | async-done | bytes 5242896 | tf_op jit(solution)/shard_map/all_gather | solution.py:21
  65.7 0.0 copy-done.3
  65.7 5.1 %fusion.5 = f32[128,2560]{0,1:T(8,128)} fusion(bf16[128,1024]{1,0:T(8,128)(2,1)S(1)} %copy-done.3, bf16[2560,1024]{1,0:T(8,128)(2,1)} %all-gather.4.cloned.1.call-done), kind=kOutput, calls=%fused_computation.15 | convolution fusion | flops 671088640 | bytes 6815744 | tf_op jit(solution)/shard_map/dot_general | solution.py:19
  70.8 0.0 reduce-scatter.2.cloned.1.call-update
  70.9 0.0 all-gather.6.cloned.1.call-start
  70.9 218.7 %all-reduce.2.cloned.1.call-done = f32[2560,128]{1,0:T(8,128)} async-done(((f32[2560,128]{1,0:T(8,128)}), f32[2560,128]{1,0:T(8,128)}) %all-reduce.2.cloned.1.call-update) | async-done | bytes 1310736 | tf_op jit(solution)/shard_map/psum | solution.py:33
  289.6 4.0 fusion.7
  293.6 0.1 copy.9
  293.8 11.7 %cholesky.16 = f32[128,128]{1,0:T(8,128)S(1)} custom-call(f32[128,128]{1,0:T(8,128)S(1)} %fusion.4), custom_call_target="Cholesky" | custom-call | tf_op jit(solution)/shard_map/jit(cholesky)/cholesky | solution.py:11
  305.5 0.6 compare_reduce_fusion
  306.1 0.7 fusion.1
  306.8 9.8 %custom-call.6 = f32[1,128,128]{1,2,0:T(8,128)S(1)} custom-call(f32[1,128,128]{2,1,0:T(8,128)S(1)} %fusion.1), custom_call_target="InvertDiagBlocksLowerTriangular" | custom-call | tf_op jit(solution)/shard_map/triangular_solve | solution.py:12
  316.6 2.5 fusion.2
  319.1 19.9 %fusion.8 = f32[1024,128]{1,0:T(8,128)} fusion(f32[2560,1024]{1,0:T(8,128)} %copy-done.1, f32[2560,128]{1,0:T(8,128)S(1)} %fusion.2), kind=kOutput, calls=%fused_computation.18 | convolution fusion | flops 4026531840 | bytes 12320768 | tf_op jit(solution)/shard_map/dot_general | solution.py:36
  339.1 0.0 all-gather.6.cloned.1.call-update
  339.1 0.0 reduce-scatter.2.cloned.1.call-done
  339.1 1.6 convert_element_type.12
  340.7 74.8 %all-gather.6.cloned.1.call-done = f32[32768,128]{1,0:T(8,128)} async-done(((f32[1024,128]{1,0:T(8,128)}), f32[32768,128]{1,0:T(8,128)}) %all-gather.6.cloned.1.call-update) | async-done | bytes 16777232 | tf_op jit(solution)/shard_map/all_gather | solution.py:7
  415.5 6.6 %reduce_sum.9 = f32[1024,128]{1,0:T(8,128)S(1)} reduce(f32[32,1024,128]{2,1,0:T(8,128)} %bitcast.28, f32[]{:T(128)} %constant.48.clone.1), dimensions={0}, to_apply=%region_4.5 | reduce | flops 4063232 | bytes 17301508 | tf_op jit(solution)/shard_map/reduce_sum | solution.py:7
  422.1 0.0 copy-start.2
  422.1 11.0 %fusion.9 = f32[2560,1024]{1,0:T(8,128)} fusion(f32[2560,128]{1,0:T(8,128)S(1)} %fusion.2, f32[1024,128]{1,0:T(8,128)S(1)} %broadcast_multiply_fusion), kind=kOutput, calls=%fused_computation.19 | convolution fusion | flops 4026531840 | bytes 12320768 | tf_op jit(solution)/shard_map/dot_general | solution.py:44
  433.1 0.0 copy-done.2
  433.1 11.6 %fusion = bf16[1,2560,1024]{2,1,0:T(8,128)(2,1)} fusion(f32[2560,1024]{1,0:T(8,128)} %copy-done.1, f32[2560,1024]{1,0:T(8,128)} %fusion.9), kind=kLoop, calls=%fused_computation.2 | loop fusion | flops 5242880 | bytes 26214400 | tf_op jit(solution)/shard_map/broadcast_in_dim | solution.py:51
  444.7 1.7 constant_dynamic-slice_fusion
  (3 shorter events, 0.1 us)
Async XLA Ops:
  8.0 1.1 copy-start
  8.0 57.7 %all-gather.4.cloned.1.call-start = ((), (), s32[]{:S(2)}) async-start(), calls=%async_computation.1 | async-start | bytes 5406720 | tf_op jit(solution)/shard_map/all_gather | solution.py:21
  8.7 8.5 %copy-start.4 = (f32[1024,128]{1,0:T(8,128)S(1)}, f32[1024,128]{1,0:T(8,128)}, u32[]{:S(2)}) copy-start(f32[1024,128]{1,0:T(8,128)} %param.9) | copy-start | bytes 1572868
  8.8 280.8 %all-reduce.2.cloned.1.call-start = ((), (), s32[]{:S(2)}) async-start(), calls=%async_computation.3 | async-start | bytes 2621440 | tf_op jit(solution)/shard_map/psum | solution.py:33
  13.2 4.0 copy-start.1
  17.2 48.5 %copy-start.3 = (bf16[128,1024]{1,0:T(8,128)(2,1)S(1)}, bf16[128,1024]{1,0:T(8,128)(2,1)}, u32[]{:S(2)}) copy-start(bf16[128,1024]{1,0:T(8,128)(2,1)} %param.6) | copy-start | bytes 786436
  26.7 312.5 %reduce-scatter.2.cloned.1.call-start = ((), (), s32[]{:S(2)}) async-start(), calls=%async_computation.2 | async-start | bytes 1474560 | tf_op jit(solution)/shard_map/reduce_scatter | solution.py:25
  70.9 344.6 %all-gather.6.cloned.1.call-start = ((), (), s32[]{:S(2)}) async-start(), calls=%async_computation.4 | async-start | bytes 17301504 | tf_op jit(solution)/shard_map/all_gather | solution.py:7
  422.1 11.1 %copy-start.2 = (f32[1024,128]{1,0:T(8,128)}, f32[1024,128]{1,0:T(8,128)S(1)}, u32[]{:S(2)}) copy-start(f32[1024,128]{1,0:T(8,128)S(1)} %broadcast_multiply_fusion) | copy-start | bytes 1572868
Sparse Core Ops, SparseCore 0:
  11.4 54.3 all-gather.3
  71.0 40.3 reduce-scatter.1
  339.2 76.2 all-gather.5
Sparse Core Ops, SparseCore 1:
  26.7 262.8 all-reduce.1
